TPU v7x, 512 devices: a whole 4x8x8 slice. The times are simulated.
512 devices in a mesh: seq: 32 (over z, x), rep: 16 (over y, core).
Axes of the slice: x: 4, y: 8, z: 8, core: 2. Of those that a mesh axis runs over, the one named last changes fastest.
Arguments:
- states: bfloat16 [98304, 512], P(('rep', 'seq')), parts along dimension 0, may hold values from -6 to 6
- starts: int32 [16384], P(('rep', 'seq')), parts along dimension 0, may hold values from 0 to 6143, as said below
- straddle: int32 [512], P(('rep', 'seq')), parts along dimension 0, may hold values from 0 to 63, as said below
- key_weight: bfloat16 [512, 512], replicated
- out_weight: bfloat16 [512, 4096], P(None, 'seq'), may hold values from -0.25 to 0.25
- norm_gain: bfloat16 [4096], P('seq'), may hold values from 0.25 to 1.75
- attn_weight: bfloat16 [4096, 3, 4096], P(None, None, 'seq')
Outputs:
- attended: bfloat16 [16384, 4096], P(('rep', 'seq')), parts along dimension 0
There are 16 independent parts, one for each index of `rep`. A program takes and returns all parts, laid end to end along the dimension named above; an argument that names none is the same for every part. Nothing has to cross between parts.
Inputs may be any that keep to these rules, and one draw needn't show every extreme that they name: Rising; shard s of 192 bytes holds the starts of exactly 32 patches, numbers s * 32 to (s+1) * 32 - 1; the first of them lies at most 63 bytes into the shard, and at byte 0 for shard 0. `straddle`: entry s equals the first start of shard s+1 minus (s+1) * 192; the last entry is 0.
All inputs are finite; a program needn't handle non-finite values.
Results may differ from a plain program's by a relative error of at most 0.0096.
Values may be sent and summed in bfloat16 or wider, within the bound.
No kernel may reach another device: no remote copies, remote signals or barrier semaphores. Data moves between devices by JAX's collectives and lax.ppermute only.
A program may use at most 64 MiB of HBM per device.

v0:
```python
import jax
import jax.numpy as jnp
from jax import lax
from jax.sharding import PartitionSpec as P

HD = 128
LHD = 128
HALO = 64
epsilon = 1e-05


def shifted(shard, axis, by):
    size = lax.axis_size(axis)
    pairs = [(i, i + by) for i in range(size) if 0 <= i + by < size]
    return lax.ppermute(shard, axis, pairs)


def cross_pool(window, local_starts, halo_count, key_weight, patch_total, head_size):
    window_rows = window.shape[0]
    shard_bytes = window_rows - HALO
    width = window.shape[1]
    head_count = width // head_size
    position = jnp.arange(window_rows, dtype=jnp.int32)
    patch_ends = jnp.concatenate([local_starts[1:], (shard_bytes + halo_count).reshape(1)])
    member = (position[None, :] >= local_starts[:, None]) & (
        position[None, :] < patch_ends[:, None]
    )
    byte_count = jnp.sum(member.astype(jnp.float32), axis=1)
    query = (
        jnp.dot(member.astype(jnp.bfloat16), window, preferred_element_type=jnp.float32)
        / byte_count[:, None]
    ).astype(jnp.bfloat16)
    keys = jnp.dot(window, key_weight, preferred_element_type=jnp.float32).astype(jnp.bfloat16)
    query_heads = query.reshape(patch_total, head_count, head_size)
    key_heads = keys.reshape(window_rows, head_count, head_size)
    scores = jnp.einsum(
        "phd,jhd->hpj", query_heads, key_heads, preferred_element_type=jnp.float32
    ) / jnp.sqrt(jnp.float32(head_size))
    scores = jnp.where(member[None], scores, jnp.float32(-1e30))
    row_peak = jnp.max(scores, axis=-1, keepdims=True)
    expo = jnp.where(member[None], jnp.exp(scores - row_peak), jnp.float32(0.0))
    cross = (expo / jnp.sum(expo, axis=-1, keepdims=True)).astype(jnp.bfloat16)
    value_heads = window.reshape(window_rows, head_count, head_size)
    pooled = jnp.einsum("hpj,jhd->phd", cross, value_heads, preferred_element_type=jnp.float32)
    return pooled.reshape(patch_total, width).astype(jnp.bfloat16)


def global_attend(head_view):
    patch_count = head_view.shape[0]
    scores = jnp.einsum(
        "qhd,khd->hqk", head_view[:, 0], head_view[:, 1], preferred_element_type=jnp.float32
    ) / jnp.sqrt(jnp.float32(HD))
    causal = jnp.arange(patch_count)[:, None] >= jnp.arange(patch_count)[None, :]
    scores = jnp.where(causal[None], scores, jnp.float32(-1e30))
    row_peak = jnp.max(scores, axis=-1, keepdims=True)
    expo = jnp.where(causal[None], jnp.exp(scores - row_peak), jnp.float32(0.0))
    probs = (expo / jnp.sum(expo, axis=-1, keepdims=True)).astype(jnp.bfloat16)
    attended = jnp.einsum(
        "hqk,khd->qhd", probs, head_view[:, 2], preferred_element_type=jnp.float32
    )
    return attended.reshape(patch_count, head_view.shape[2] * HD).astype(jnp.bfloat16)


def norm_rows(embedding, gain_row):
    meansq = jnp.mean(embedding * embedding, axis=1, keepdims=True)
    return (embedding * lax.rsqrt(meansq + epsilon) * gain_row.astype(jnp.float32)).astype(
        jnp.bfloat16
    )


def shards(states, starts, straddle, key_weight, out_weight, norm_gain, attn_weight):
    shard_index = lax.axis_index("seq")
    byte_rows = states.shape[0]
    patch_local = starts.shape[0]
    halo_rows = shifted(states[:HALO], "seq", -1)
    window = jnp.concatenate([states, halo_rows], axis=0)
    local_starts = starts - shard_index * byte_rows
    pooled = cross_pool(window, local_starts, straddle[0], key_weight, patch_local, LHD)
    local_width = attn_weight.shape[2]
    model_width = attn_weight.shape[0]
    proj_weight = attn_weight.reshape(model_width, 3 * local_width)
    out_full, gain_full = (
        lax.all_gather(out_weight, "seq", axis=1, tiled=True),
        lax.all_gather(norm_gain.reshape(1, -1), "seq", axis=1, tiled=True),
    )
    embedding = jnp.dot(pooled, out_full, preferred_element_type=jnp.float32)
    normed = norm_rows(embedding, gain_full)
    projected = jnp.dot(
        lax.all_gather(normed, "seq", axis=0, tiled=True),
        proj_weight,
        preferred_element_type=jnp.float32,
    ).astype(jnp.bfloat16)
    head_view = projected.reshape(projected.shape[0], 3, local_width // HD, HD)
    attended = global_attend(head_view)
    return lax.all_to_all(attended, "seq", split_axis=0, concat_axis=1, tiled=True)


def solution(mesh):
    placed = (
        P(("rep", "seq"), None),
        P(("rep", "seq")),
        P(("rep", "seq")),
        P(),
        P(None, "seq"),
        P("seq"),
        P(None, None, "seq"),
    )
    return jax.shard_map(
        shards, mesh=mesh, in_specs=placed, out_specs=P(("rep", "seq"), None), check_vma=False
    )
```

profile of v0, /device:TPU:8, one launch (start us, length us, event | category | flops | bytes accessed | tf_op | source)
XLA Modules:
  0.0 247.6 jit_solution(9140741254961553201)
XLA Ops:
  6.5 0.0 copy-start
  6.5 0.0 all-gather.5.cloned.1.call-start
  6.5 0.7 all-gather.5.cloned.1.call-update
  7.3 0.0 all-gather.7.cloned.1.call-start
  7.3 1.1 copy.29
  8.4 1.3 collective-permute-start
  10.3 0.7 broadcast_subtract_fusion
  11.0 0.1 slice.16
  11.1 46.9 %all-gather.1 = bf16[32,1,128]{2,1,0:T(2,128)(2,1)S(1)} all-gather(bf16[1,1,128]{2,1,0:T(2,128)(2,1)} %bitcast.62), channel_id=2, replica_groups=mesh['seq'=32,'rep'=16] {'seq'}, dimensions={0}, use_global_device_ids=true | all-gather | bytes 8448 | tf_op jit(solution)/shard_map/all_gather | solution.py:84
  58.0 0.1 pad_add_fusion
  58.1 0.1 fusion.23
  58.2 0.2 convert_reduce_fusion
  58.4 0.0 collective-permute-done
  58.4 0.1 pad_maximum_fusion
  58.5 0.2 fusion.13
  58.7 0.0 copy-done
  58.7 0.3 fusion.5
  59.0 0.4 fusion.28
  59.4 0.2 fusion.12
  59.6 44.0 %all-gather.5.cloned.1.call-done = bf16[512,4096]{1,0:T(8,128)(2,1)} async-done(((bf16[512,128]{1,0:T(8,128)(2,1)}), bf16[512,4096]{1,0:T(8,128)(2,1)}) %all-gather.5.cloned.1.call-update) | async-done | bytes 4194320 | tf_op jit(solution)/shard_map/all_gather | solution.py:83
  103.7 3.1 %multiply_reduce_fusion = (f32[32]{0:T(128)S(1)}, f32[32,4096]{1,0:T(8,128)S(1)}) fusion(bf16[512,4096]{1,0:T(8,128)(2,1)} %all-gather.5.cloned.1.call-done, bf16[4,4,8,128]{3,2,1,0:T(8,128)(2,1)S(1)} %fusion.12), kind=kOutput, calls=%fused_computation.24 | convolution fusion | flops 134479840 | bytes 4751488 | tf_op jit(solution)/shard_map/dot_general | solution.py:86
  106.8 0.8 multiply_convert_fusion
  107.7 0.0 all-gather.7.cloned.1.call-update
  107.7 4.7 %copy.34 = bf16[4096,3,128]{0,2,1:T(8,128)(2,1)} copy(bf16[4096,3,128]{2,0,1:T(8,128)(2,1)} %param.13) | data formatting | bytes 6291456 | tf_op args[6]
  112.4 100.1 %all-gather.7.cloned.1.call-done = bf16[1024,4096]{1,0:T(8,128)(2,1)} async-done(((bf16[32,4096]{1,0:T(8,128)(2,1)}), bf16[1024,4096]{1,0:T(8,128)(2,1)}) %all-gather.7.cloned.1.call-update) | async-done | bytes 8388624 | tf_op jit(solution)/shard_map/all_gather | solution.py:89
  212.5 7.7 %convolution_convert_fusion = bf16[1024,384]{0,1:T(8,128)(2,1)S(1)} fusion(bf16[1024,4096]{1,0:T(8,128)(2,1)} %all-gather.7.cloned.1.call-done, bf16[4096,384]{0,1:T(8,128)(2,1)} %bitcast.58), kind=kOutput, calls=%fused_computation.8 | convolution fusion | flops 3221618688 | bytes 12320768 | tf_op jit(solution)/shard_map/dot_general | solution.py:88
  220.2 0.8 fusion.1
  220.9 0.5 fusion.2
  221.4 0.8 fusion.6
  222.2 0.2 copy.35
  222.3 17.7 %all_to_all.16 = bf16[32,32,128]{2,1,0:T(8,128)(2,1)S(1)} all-to-all(bf16[32,32,128]{2,1,0:T(8,128)(2,1)S(1)} %bitcast.59), channel_id=1, replica_groups=mesh['seq'=32,'rep'=16] {'seq'}, dimensions={0} | all-to-all | bytes 524288 | tf_op jit(solution)/shard_map/all_to_all | solution.py:95
  240.0 0.7 copy_bitcast_fusion
  (3 shorter events, 0.0 us)
Async XLA Ops:
  6.5 52.2 %copy-start = (bf16[512,512]{1,0:T(8,128)(2,1)S(1)}, bf16[512,512]{1,0:T(8,128)(2,1)}, u32[]{:S(2)}) copy-start(bf16[512,512]{1,0:T(8,128)(2,1)} %param.10) | copy-start | bytes 1572868
  6.5 97.1 %all-gather.5.cloned.1.call-start = ((), (), s32[]{:S(2)}) async-start(), calls=%async_computation.1 | async-start | bytes 4325376 | tf_op jit(solution)/shard_map/all_gather | solution.py:83
  7.3 205.2 %all-gather.7.cloned.1.call-start = ((), (), s32[]{:S(2)}) async-start(), calls=%async_computation.2 | async-start | bytes 8650752 | tf_op jit(solution)/shard_map/all_gather | solution.py:89
  8.4 50.0 %collective-permute-start = (bf16[64,512]{0,1:T(8,128)(2,1)S(1)}, bf16[64,512]{0,1:T(8,128)(2,1)S(1)}, u32[]{:S(2)}, u32[]{:S(2)}) collective-permute-start(bf16[64,512]{0,1:T(8,128)(2,1)S(1)} %slice.20), channel_id=1, source_target_pairs={{16,0},{32,16},{48,32},{64,48},{80,64},{96,80},{112,96},{128,112},... | collective-permute-start | bytes 196616 | tf_op jit(solution)/shard_map/ppermute | solution.py:15
Sparse Core Ops, SparseCore 0:
  10.4 93.2 all-gather.4
  107.8 104.6 all-gather.6
where the time goes:
time: 248 us
  waiting for transfers between devices  145 us (58%)
  blocking collectives  64.6 us (26%)
  between operations  14.2 us (6%)
  matrix products  13.4 us (5%)
  local copies, waits for them, and re-layouts  6.75 us (3%)
    all_gather x1, waiting for transfers between devices, shards(): lax.all_gather(normed, 'seq', axis=0, tiled=True)  100 us
    all_gather x1, blocking collectives, shards(): lax.all_gather(norm_gain.reshape(1, -1), 'seq', axis=1, tiled=True)  46.9 us
    all_gather x1, waiting for transfers between devices, shards(): lax.all_gather(out_weight, 'seq', axis=1, tiled=True)  44 us
    all_to_all x1, blocking collectives, shards(): lax.all_to_all(attended, 'seq', split_axis=0, concat_axis=1, tiled=True)  17.7 us
    dot_general x1, matrix products, shards(): jnp.dot(lax.all_gather(normed, 'seq', axis=0, tiled=True), proj_weight, p...  7.71 us
    unnamed x4, local copies, waits for them, and re-layouts  5.78 us
  transfers between devices with their start and end apart: 3, of which 2 were waited for; matrix products, arithmetic and copies ran while one was open for 3% of the time, Pallas kernels for 0%

commit v1 on v0

--- a/solution.py
+++ b/solution.py
@@ -2,6 +2,7 @@
 import jax.numpy as jnp
 from jax import lax
 from jax.sharding import PartitionSpec as P
+from jax.lax import all_to_all, psum
 
 HD = 128
 LHD = 128
@@ -69,6 +70,12 @@
 
 
 def shards(states, starts, straddle, key_weight, out_weight, norm_gain, attn_weight):
+
+    def link_the_tails(z_in):
+        newest = jnp.stack([z_in] * psum(1, "seq"))
+        moved = jnp.concatenate(all_to_all(newest, "seq", 0, 0), 1)
+        return moved
+
     shard_index = lax.axis_index("seq")
     byte_rows = states.shape[0]
     patch_local = starts.shape[0]
@@ -80,7 +87,7 @@
     model_width = attn_weight.shape[0]
     proj_weight = attn_weight.reshape(model_width, 3 * local_width)
     out_full, gain_full = (
-        lax.all_gather(out_weight, "seq", axis=1, tiled=True),
+        link_the_tails(out_weight),
         lax.all_gather(norm_gain.reshape(1, -1), "seq", axis=1, tiled=True),
     )
     embedding = jnp.dot(pooled, out_full, preferred_element_type=jnp.float32)

time: 248 us -> 293 us (1.18)
  blocking collectives: 64.6 us -> 142 us
  waiting for transfers between devices: 145 us -> 97.1 us
  starting transfers between devices: 1.33 us -> 14.8 us
    all_gather x1, blocking collectives: 46.9 us -> 124 us  [shards(): lax.all_gather(norm_gain.reshape(1, -1), 'seq', axis=1, tiled=True)]
    all_gather x1 -> x0, waiting for transfers between devices: 44 us -> none  [shards(): lax.all_gather(out_weight, 'seq', axis=1, tiled=True)]
    all_to_all x0 -> x1, starting transfers between devices: none -> 13.4 us  [link_the_tails(): moved = jnp.concatenate(all_to_all(newest, 'seq', 0, 0), 1)]
    all_gather x1, waiting for transfers between devices: 100 us -> 97 us  [shards(): lax.all_gather(normed, 'seq', axis=0, tiled=True)]
    unnamed x4 -> x11, local copies, waits for them, and re-layouts: 5.78 us -> 5.93 us
  transfers between devices with their start and end apart: 3 -> 3, of which waited for: 2 -> 1; matrix products, arithmetic and copies ran while one was open for 3% -> 2% of each run, Pallas kernels for 0% -> 0%
where the time goes in v1:
time: 293 us
  blocking collectives  142 us (48%)
  waiting for transfers between devices  97.1 us (33%)
  starting transfers between devices  14.8 us (5%)
  between operations  14.2 us (5%)
  matrix products  13.9 us (5%)
  local copies, waits for them, and re-layouts  9.34 us (3%)
    all_gather x1, blocking collectives, shards(): lax.all_gather(norm_gain.reshape(1, -1), 'seq', axis=1, tiled=True)  124 us
    all_gather x1, waiting for transfers between devices, shards(): lax.all_gather(normed, 'seq', axis=0, tiled=True)  97 us
    all_to_all x1, blocking collectives, shards(): lax.all_to_all(attended, 'seq', split_axis=0, concat_axis=1, tiled=True)  17.7 us
    all_to_all x1, starting transfers between devices, link_the_tails(): moved = jnp.concatenate(all_to_all(newest, 'seq', 0, 0), 1)  13.4 us
    dot_general x1, matrix products, shards(): jnp.dot(lax.all_gather(normed, 'seq', axis=0, tiled=True), proj_weight, p...  7.71 us
    unnamed x11, local copies, waits for them, and re-layouts  5.93 us
  transfers between devices with their start and end apart: 3, of which 1 were waited for; matrix products, arithmetic and copies ran while one was open for 2% of the time, Pallas kernels for 0%

profile of v1, /device:TPU:8, one launch (start us, length us, event | category | flops | bytes accessed | tf_op | source)
XLA Modules:
  0.0 292.9 jit_solution(9941015017267827045)
XLA Ops:
  6.5 0.0 copy-start
  6.5 1.1 copy.36
  7.6 2.4 stack.2
  10.1 0.0 copy-start.1
  10.1 0.0 copy-start.3
  10.1 0.0 copy-start.2
  10.1 13.4 %all-to-all-start = ((bf16[32,512,128]{1,2,0:T(8,128)(2,1)}), bf16[32,512,128]{1,2,0:T(8,128)(2,1)}, u32[]{:S(2)}, u32[]{:S(2)}) async-start(bf16[32,512,128]{1,2,0:T(8,128)(2,1)} %stack.2), calls=%async_computation | async-start | bytes 8388608 | tf_op jit(solution)/shard_map/all_to_all | solution.py:76
  23.5 0.0 all-gather.4.cloned.1.call-start
  23.5 0.0 copy-done.1
  23.6 0.1 copy.31
  23.7 1.3 collective-permute-start
  25.7 0.0 copy-done.3
  25.7 0.1 slice.16
  25.8 0.0 copy-done.2
  25.8 124.1 %all-gather.1 = bf16[32,1,128]{2,1,0:T(2,128)(2,1)S(1)} all-gather(bf16[1,1,128]{2,1,0:T(2,128)(2,1)S(1)} %bitcast.65), channel_id=2, replica_groups=mesh['seq'=32,'rep'=16] {'seq'}, dimensions={0}, use_global_device_ids=true | all-gather | bytes 8448 | tf_op jit(solution)/shard_map/all_gather | solution.py:91
  149.8 0.1 pad_add_fusion
  149.9 0.1 fusion.23
  150.0 0.2 convert_reduce_fusion
  150.2 0.0 collective-permute-done
  150.2 0.1 pad_maximum_fusion
  150.3 0.2 fusion.13
  150.5 0.0 copy-done
  150.5 0.3 fusion.5
  150.9 0.4 fusion.28
  151.2 0.2 fusion.12
  151.4 0.0 all-to-all-done
  151.5 3.6 %multiply_reduce_fusion = (f32[32]{0:T(128)S(1)}, f32[32,4096]{1,0:T(8,128)S(1)}) fusion(bf16[512,4096]{0,1:T(8,128)(2,1)} %bitcast.3, bf16[4,4,8,128]{3,2,1,0:T(8,128)(2,1)S(1)} %fusion.12), kind=kOutput, calls=%fused_computation.24 | convolution fusion | flops 134479840 | bytes 4751488 | tf_op jit(solution)/shard_map/dot_general | solution.py:93
  155.1 0.8 multiply_convert_fusion
  155.9 0.0 all-gather.4.cloned.1.call-update
  156.0 4.7 %copy.37 = bf16[4096,3,128]{0,2,1:T(8,128)(2,1)} copy(bf16[4096,3,128]{2,0,1:T(8,128)(2,1)} %param.13) | data formatting | bytes 6291456 | tf_op args[6]
  160.7 97.0 %all-gather.4.cloned.1.call-done = bf16[1024,4096]{1,0:T(8,128)(2,1)} async-done(((bf16[32,4096]{1,0:T(8,128)(2,1)}), bf16[1024,4096]{1,0:T(8,128)(2,1)}) %all-gather.4.cloned.1.call-update) | async-done | bytes 8388624 | tf_op jit(solution)/shard_map/all_gather | solution.py:96
  257.7 7.7 %convolution_convert_fusion = bf16[1024,384]{0,1:T(8,128)(2,1)S(1)} fusion(bf16[1024,4096]{1,0:T(8,128)(2,1)} %all-gather.4.cloned.1.call-done, bf16[4096,384]{0,1:T(8,128)(2,1)} %bitcast.61), kind=kOutput, calls=%fused_computation.8 | convolution fusion | flops 3221618688 | bytes 12320768 | tf_op jit(solution)/shard_map/dot_general | solution.py:95
  265.4 0.8 fusion.1
  266.2 0.5 fusion.2
  266.7 0.8 fusion.6
  267.4 0.2 copy.38
  267.6 17.7 %all_to_all.21 = bf16[32,32,128]{2,1,0:T(8,128)(2,1)S(1)} all-to-all(bf16[32,32,128]{2,1,0:T(8,128)(2,1)S(1)} %bitcast.62), channel_id=1, replica_groups=mesh['seq'=32,'rep'=16] {'seq'}, dimensions={0} | all-to-all | bytes 524288 | tf_op jit(solution)/shard_map/all_to_all | solution.py:102
  285.3 0.7 copy_bitcast_fusion
  (4 shorter events, 0.0 us)
Async XLA Ops:
  6.5 144.0 %copy-start = (bf16[512,512]{1,0:T(8,128)(2,1)S(1)}, bf16[512,512]{1,0:T(8,128)(2,1)}, u32[]{:S(2)}) copy-start(bf16[512,512]{1,0:T(8,128)(2,1)} %param.10) | copy-start | bytes 1572868
  10.1 13.5 %copy-start.1 = (bf16[192,512]{1,0:T(8,128)(2,1)S(1)}, bf16[192,512]{1,0:T(8,128)(2,1)}, u32[]{:S(2)}) copy-start(bf16[192,512]{1,0:T(8,128)(2,1)} %param.7) | copy-start | bytes 589828
  10.1 15.6 %copy-start.3 = (s32[32]{0:T(128)S(1)}, s32[32]{0:T(128)}, u32[]{:S(2)}) copy-start(s32[32]{0:T(128)} %param.8) | copy-start | bytes 388
  10.1 15.7 %copy-start.2 = (bf16[128]{0:T(256)(128)(2,1)S(1)}, bf16[128]{0:T(256)(128)(2,1)}, u32[]{:S(2)}) copy-start(bf16[128]{0:T(256)(128)(2,1)} %param.12) | copy-start | bytes 772
  10.1 141.4 %all-to-all-start = ((bf16[32,512,128]{1,2,0:T(8,128)(2,1)}), bf16[32,512,128]{1,2,0:T(8,128)(2,1)}, u32[]{:S(2)}, u32[]{:S(2)}) async-start(bf16[32,512,128]{1,2,0:T(8,128)(2,1)} %stack.2), calls=%async_computation | async-start | bytes 8388608 | tf_op jit(solution)/shard_map/all_to_all | solution.py:76
  23.5 234.2 %all-gather.4.cloned.1.call-start = ((), (), s32[]{:S(2)}) async-start(), calls=%async_computation.2 | async-start | bytes 8650752 | tf_op jit(solution)/shard_map/all_gather | solution.py:96
  23.7 126.5 %collective-permute-start = (bf16[64,512]{0,1:T(8,128)(2,1)S(1)}, bf16[64,512]{0,1:T(8,128)(2,1)S(1)}, u32[]{:S(2)}, u32[]{:S(2)}) collective-permute-start(bf16[64,512]{0,1:T(8,128)(2,1)S(1)} %slice.20), channel_id=1, source_target_pairs={{16,0},{32,16},{48,32},{64,48},{80,64},{96,80},{112,96},{128,112},... | collective-permute-start | bytes 196616 | tf_op jit(solution)/shard_map/ppermute | solution.py:16
Sparse Core Ops, SparseCore 0:
  156.1 101.5 all-gather.3
